TPU v7x, 512 devices: a whole 4x8x8 slice. The times are simulated.
512 devices in a mesh: expert: 64 (over y, x, core), hidden: 8 (over z).
Axes of the slice: x: 4, y: 8, z: 8, core: 2. Of those that a mesh axis runs over, the one named last changes fastest.
Arguments:
- tokens: bfloat16 [4096, 4096], P('expert', 'hidden'), may hold values from -6 to 6
- expert_ids: int32 [4096, 8], P('expert'), may hold values from 0 to 63, all different within a row; in each aligned block of 64 rows (0 to 63, 64 to 127, ...) at most 16 rows name the same one
- gate_weights: float32 [4096, 8], P('expert'), may hold values from 0.05 to 0.5
- gate_proj: bfloat16 [64, 1536, 4096], P('expert', 'hidden'), may hold values from -0.09375 to 0.09375
- up_proj: bfloat16 [64, 1536, 4096], P('expert', 'hidden'), may hold values from -0.09375 to 0.09375
- down_proj: bfloat16 [64, 1536, 4096], P('expert', None, 'hidden'), may hold values from -0.15625 to 0.15625
Outputs:
- moe_out: bfloat16 [4096, 4096], P('expert', 'hidden')
Inputs may be any that keep to these rules, and one draw needn't show every extreme that they name: `expert_ids`: each row names 8 different experts; in each aligned block of 64 rows no expert is named by more than 16 rows.
All inputs are finite; a program needn't handle non-finite values.
Results may differ from a plain program's by a relative error of at most 0.0057.
Values may be sent and summed in bfloat16 or wider, within the bound.
No kernel may reach another device: no remote copies, remote signals or barrier semaphores. Data moves between devices by JAX's collectives and lax.ppermute only.
A program may use at most 64 MiB of HBM per device.

v0:
```python
import jax
import jax.numpy as jnp
from jax import lax
from jax.sharding import PartitionSpec as P


def on_device(tokens, expert_ids, gate_weights, gate_proj, up_proj, down_proj):
    local_count = gate_proj.shape[0]
    experts_all = local_count * lax.axis_size("expert")
    tok_rows = tokens.shape[0]
    top_count = expert_ids.shape[1]
    capacity = 2 * tok_rows * top_count // experts_all
    flat_ids = expert_ids.reshape(-1)
    onehot = (flat_ids[:, None] == jnp.arange(experts_all, dtype=jnp.int32)[None, :]).astype(
        jnp.int32
    )
    slot_index = jnp.sum((jnp.cumsum(onehot, axis=0) - onehot) * onehot, axis=1)
    position = flat_ids * capacity + slot_index
    token_of = jnp.arange(tok_rows * top_count, dtype=jnp.int32) // top_count
    full_rows = lax.all_gather(tokens, "hidden", axis=1, tiled=True)
    packed = jnp.zeros((experts_all * capacity, full_rows.shape[1]), full_rows.dtype)
    packed = packed.at[position].set(full_rows[token_of])
    arrived = lax.all_to_all(
        packed.reshape(experts_all, capacity, full_rows.shape[1]),
        "expert",
        split_axis=0,
        concat_axis=1,
        tiled=True,
    )
    gate_sum = jnp.einsum("lrd,lfd->lfr", arrived, gate_proj, preferred_element_type=jnp.float32)
    up_sum = jnp.einsum("lrd,lfd->lfr", arrived, up_proj, preferred_element_type=jnp.float32)
    activation = (jax.nn.silu(gate_sum) * up_sum).astype(jnp.bfloat16)
    expert_out = jnp.einsum(
        "lfr,lfd->lrd",
        lax.all_gather(activation, "hidden", axis=1, tiled=True),
        down_proj,
        preferred_element_type=jnp.float32,
    ).astype(jnp.bfloat16)
    returned = lax.all_to_all(expert_out, "expert", split_axis=1, concat_axis=0, tiled=True)
    gathered = returned.reshape(experts_all * capacity, returned.shape[2])[position]
    gathered = gathered.reshape(tok_rows, top_count, returned.shape[2]).astype(jnp.float32)
    mixed = jnp.sum(gathered * gate_weights[:, :, None], axis=1)
    return mixed.astype(jnp.bfloat16)


def solution(mesh):
    in_specs = (
        P("expert", "hidden"),
        P("expert", None),
        P("expert", None),
        P("expert", "hidden", None),
        P("expert", "hidden", None),
        P("expert", None, "hidden"),
    )
    out_specs = P("expert", "hidden")
    return jax.shard_map(
        on_device, mesh=mesh, in_specs=in_specs, out_specs=out_specs, check_vma=False
    )
```

profile of v0, /device:TPU:1, one launch (start us, length us, event | category | flops | bytes accessed | tf_op | source)
XLA Modules:
  0.0 375.7 jit_solution(17025929349063810798)
XLA Ops:
  6.5 0.9 copy.20
  7.6 0.7 broadcast_multiply_fusion
  8.3 1.2 reduce-window.6
  9.5 0.2 slice_reduce_fusion
  9.9 0.1 mul.38
  10.0 27.1 %all_gather.6 = bf16[64,4096]{1,0:T(8,128)(2,1)S(1)} all-gather(bf16[64,512]{1,0:T(8,128)(2,1)} %param.6), channel_id=1, replica_groups=mesh['expert'=64,'hidden'=8] {'hidden'}, dimensions={1}, use_global_device_ids=true | all-gather | bytes 589824 | tf_op jit(solution)/shard_map/all_gather | solution.py:20
  37.1 0.1 fusion.29
  37.3 4.4 %gather_fusion = bf16[512,4096]{1,0:T(8,128)(2,1)} fusion(bf16[64,4096]{1,0:T(8,128)(2,1)S(1)} %all_gather.6, s32[1024]{0:T(1024)S(1)} %pad_clamp_fusion.1), kind=kCustom, calls=%fused_computation | custom fusion | bytes 8390656 | tf_op jit(solution)/shard_map/gather | solution.py:22
  41.6 12.4 %scatter_custom_fusion = bf16[1024,4096]{1,0:T(8,128)(2,1)} fusion(s32[512]{0:T(512)S(1)} %bitcast.75, bf16[512,4096]{1,0:T(8,128)(2,1)} %gather_fusion, bf16[]{:T(256)} %constant.26.clone.1), kind=kCustom, calls=%fused_computation.3 | custom fusion | bytes 8389120 | tf_op jit(solution)/shard_map/scatter | solution.py:22
  54.1 201.0 %all_to_all.8 = bf16[64,16,4096]{2,1,0:T(8,128)(2,1)S(1)} all-to-all(bf16[64,16,4096]{2,1,0:T(8,128)(2,1)} %bitcast.68), channel_id=1, replica_groups=mesh['expert'=64,'hidden'=8] {'expert'}, dimensions={0} | all-to-all | bytes 16777216 | tf_op jit(solution)/shard_map/all_to_all | solution.py:23
  255.0 2.9 fusion.14
  258.0 3.7 fusion.23
  261.7 43.4 %all-gather.3.cloned.1.call-done = bf16[1536,1024]{1,0:T(8,128)(2,1)} async-done(((bf16[192,1024]{1,0:T(8,128)(2,1)}), bf16[1536,1024]{1,0:T(8,128)(2,1)}) %all-gather.3.cloned.1.call-update) | async-done | bytes 3145744 | tf_op jit(solution)/shard_map/all_gather | solution.py:35
  305.1 3.7 fusion.11
  308.8 3.0 copy.31
  311.8 0.5 broadcast.125
  312.3 8.3 %reduce.2 = bf16[1024,512]{1,0:T(8,128)(2,1)S(1)} reduce(bf16[1024,1,512]{2,1,0:T(2,128)(2,1)} %bitcast.73, bf16[]{:T(256)} %broadcast.125), dimensions={1}, to_apply=%bitcast.67.reduce_sub_computation | reduce | bytes 2097154
  320.6 1.6 reshape.173
  322.2 10.3 %all-to-all-start.1 = ((bf16[64,2,4096]{2,1,0:T(2,128)(2,1)}), bf16[64,2,4096]{2,1,0:T(2,128)(2,1)S(1)}, u32[]{:S(2)}, u32[]{:S(2)}) async-start(bf16[64,2,4096]{2,1,0:T(2,128)(2,1)} %reshape.173), calls=%async_computation.1 | async-start | bytes 2097152 | tf_op jit(solution)/shard_map/all_to_all | solution.py:39
  332.6 27.9 %all-to-all-done.1 = bf16[64,2,4096]{2,1,0:T(2,128)(2,1)S(1)} async-done(((bf16[64,2,4096]{2,1,0:T(2,128)(2,1)}), bf16[64,2,4096]{2,1,0:T(2,128)(2,1)S(1)}, u32[]{:S(2)}, u32[]{:S(2)}) %all-to-all-start.1) | async-done | bytes 1048608 | tf_op jit(solution)/shard_map/all_to_all | solution.py:39
  360.5 3.5 reshape.174
  364.0 1.9 copy.30
  365.9 2.0 gather_fusion.1
  367.8 1.0 fusion.26
  (21 shorter events, 0.5 us)
Async XLA Ops:
  6.5 298.6 %copy-start = (bf16[1,1536,512]{2,1,0:T(8,128)(2,1)S(1)}, bf16[1,1536,512]{2,1,0:T(8,128)(2,1)}, u32[]{:S(2)}) copy-start(bf16[1,1536,512]{2,1,0:T(8,128)(2,1)} %param.11) | copy-start | bytes 4718596
  6.5 298.6 %all-gather.3.cloned.1.call-start = ((), (), s32[]{:S(2)}) async-start(), calls=%async_computation.2 | async-start | bytes 3538944 | tf_op jit(solution)/shard_map/all_gather | solution.py:35
  54.1 201.0 %copy-start.2 = (bf16[1,192,4096]{2,1,0:T(8,128)(2,1)S(1)}, bf16[1,192,4096]{2,1,0:T(8,128)(2,1)}, u32[]{:S(2)}) copy-start(bf16[1,192,4096]{2,1,0:T(8,128)(2,1)} %param.9) | copy-start | bytes 4718596
  255.0 2.9 copy-start.3
  311.8 20.7 %copy-start.1 = (f32[64,8]{0,1:T(8,128)S(1)}, f32[64,8]{0,1:T(8,128)}, u32[]{:S(2)}) copy-start(f32[64,8]{0,1:T(8,128)} %param.8) | copy-start | bytes 6148
  322.2 38.3 %all-to-all-start.1 = ((bf16[64,2,4096]{2,1,0:T(2,128)(2,1)}), bf16[64,2,4096]{2,1,0:T(2,128)(2,1)S(1)}, u32[]{:S(2)}, u32[]{:S(2)}) async-start(bf16[64,2,4096]{2,1,0:T(2,128)(2,1)} %reshape.173), calls=%async_computation.1 | async-start | bytes 2097152 | tf_op jit(solution)/shard_map/all_to_all | solution.py:39
Sparse Core Ops, SparseCore 0:
  261.8 43.2 all-gather.2
where the time goes:
time: 376 us
  blocking collectives  228 us (61%)
  waiting for transfers between devices  71.3 us (19%)
  local copies, waits for them, and re-layouts  30.8 us (8%)
  between operations  13.5 us (4%)
  other arithmetic  11.3 us (3%)
  starting transfers between devices  10.4 us (3%)
  matrix products  10.3 us (3%)
    all_to_all x1, blocking collectives, on_device(): lax.all_to_all(packed.reshape(experts_all, capacity, full_rows.shape[1]),...  201 us
    all_gather x1, waiting for transfers between devices, on_device(): lax.all_gather(activation, 'hidden', axis=1, tiled=True)  43.4 us
    all_to_all x1, waiting for transfers between devices, on_device(): lax.all_to_all(expert_out, 'expert', split_axis=1, concat_axis=0, tiled=T...  27.9 us
    all_gather x1, blocking collectives, on_device(): full_rows = lax.all_gather(tokens, 'hidden', axis=1, tiled=True)  27.1 us
    scatter x1, local copies, waits for them, and re-layouts, on_device(): packed = packed.at[position].set(full_rows[token_of])  12.4 us
    all_to_all x1, starting transfers between devices, on_device(): lax.all_to_all(expert_out, 'expert', split_axis=1, concat_axis=0, tiled=T...  10.3 us
    unnamed x14, local copies, waits for them, and re-layouts  8.43 us
    unnamed x1, other arithmetic  8.25 us
  transfers between devices with their start and end apart: 2, of which 2 were waited for; matrix products, arithmetic and copies ran while one was open for 0% of the time, Pallas kernels for 0%

commit v1 on v0

--- a/solution.py
+++ b/solution.py
@@ -2,6 +2,27 @@
 import jax.numpy as jnp
 from jax import lax
 from jax.sharding import PartitionSpec as P
+
+
+def ring_gather(x, axis, dim):
+    size, index, width = (lax.axis_size(axis), lax.axis_index(axis), x.shape[dim])
+    right = [(i, (i + 1) % size) for i in range(size)]
+    left = [(i, (i - 1) % size) for i in range(size)]
+    out = jnp.zeros((*x.shape[:dim], size * width, *x.shape[dim + 1 :]), x.dtype)
+    out = lax.dynamic_update_slice_in_dim(out, x, index * width, axis=dim)
+    from_left = from_right = x
+    middle = size // 2
+    for step in range(1, middle + 1):
+        from_left = lax.ppermute(from_left, axis, right)
+        out = lax.dynamic_update_slice_in_dim(
+            out, from_left, (index - step) % size * width, axis=dim
+        )
+        if step < size - middle:
+            from_right = lax.ppermute(from_right, axis, left)
+            out = lax.dynamic_update_slice_in_dim(
+                out, from_right, (index + step) % size * width, axis=dim
+            )
+    return out
 
 
 def on_device(tokens, expert_ids, gate_weights, gate_proj, up_proj, down_proj):
@@ -32,7 +53,7 @@
     activation = (jax.nn.silu(gate_sum) * up_sum).astype(jnp.bfloat16)
     expert_out = jnp.einsum(
         "lfr,lfd->lrd",
-        lax.all_gather(activation, "hidden", axis=1, tiled=True),
+        ring_gather(activation, "hidden", 1),
         down_proj,
         preferred_element_type=jnp.float32,
     ).astype(jnp.bfloat16)

time: 376 us -> 381 us (1.013)
  blocking collectives: 228 us -> 27.1 us
  waiting for transfers between devices: 71.3 us -> 225 us
  starting transfers between devices: 10.4 us -> 60.7 us
  between operations: 13.5 us -> 0.3 us
  local copies, waits for them, and re-layouts: 30.8 us -> 38.5 us
  matrix products: 10.3 us -> 17.5 us
    all_to_all x1 -> x0, blocking collectives: 201 us -> none  [on_device(): lax.all_to_all(packed.reshape(experts_all, capacity, full_rows.shape[1]),...]
    all_to_all x0 -> x1, waiting for transfers between devices: none -> 182 us  [on_device(): lax.all_to_all(packed.reshape(experts_all, capacity, full_rows.shape[1]),...]
    all_gather x1 -> x0, waiting for transfers between devices: 43.4 us -> none  [on_device(): lax.all_gather(activation, 'hidden', axis=1, tiled=True)]
    ppermute x0 -> x7, starting transfers between devices: none -> 21.1 us  [the longest x3 11.7 us: ring_gather(): from_right = lax.ppermute(from_right, axis, left)]
    all_to_all x0 -> x1, starting transfers between devices: none -> 16.7 us  [on_device(): lax.all_to_all(packed.reshape(experts_all, capacity, full_rows.shape[1]),...]
    ppermute x0 -> x7, waiting for transfers between devices: none -> 14.5 us  [the longest x4 14.2 us: ring_gather(): from_left = lax.ppermute(from_left, axis, right)]
    all_to_all x1, starting transfers between devices: 10.3 us -> 22.9 us  [on_device(): lax.all_to_all(expert_out, 'expert', split_axis=1, concat_axis=0, tiled=T...]
    dynamic_update_slice x0 -> x7, local copies, waits for them, and re-layouts: none -> 5.56 us  [the longest x4 3.17 us: ring_gather(): lax.dynamic_update_slice_in_dim(out, from_left, (index - step) % size * w...]
  transfers between devices with their start and end apart: 2 -> 9, of which waited for: 2 -> 7; matrix products, arithmetic and copies ran while one was open for 0% -> 1% of each run, Pallas kernels for 0% -> 0%
where the time goes in v1:
time: 381 us; the launch traced here: 380 us
  waiting for transfers between devices  225 us (59%)
  starting transfers between devices  60.7 us (16%)
  local copies, waits for them, and re-layouts  38.5 us (10%)
  blocking collectives  27.1 us (7%)
  matrix products  17.5 us (5%)
  other arithmetic  11.1 us (3%)
    all_to_all x1, waiting for transfers between devices, on_device(): lax.all_to_all(packed.reshape(experts_all, capacity, full_rows.shape[1]),...  182 us
    all_to_all x1, waiting for transfers between devices, on_device(): lax.all_to_all(expert_out, 'expert', split_axis=1, concat_axis=0, tiled=T...  27.9 us
    all_gather x1, blocking collectives, on_device(): full_rows = lax.all_gather(tokens, 'hidden', axis=1, tiled=True)  27.1 us
    all_to_all x1, starting transfers between devices, on_device(): lax.all_to_all(expert_out, 'expert', split_axis=1, concat_axis=0, tiled=T...  22.9 us
    all_to_all x1, starting transfers between devices, on_device(): lax.all_to_all(packed.reshape(experts_all, capacity, full_rows.shape[1]),...  16.7 us
    ppermute x4, waiting for transfers between devices, ring_gather(): from_left = lax.ppermute(from_left, axis, right)  14.2 us
    scatter x1, local copies, waits for them, and re-layouts, on_device(): packed = packed.at[position].set(full_rows[token_of])  12.4 us
    ppermute x3, starting transfers between devices, ring_gather(): from_right = lax.ppermute(from_right, axis, left)  11.7 us
  transfers between devices with their start and end apart: 9, of which 7 were waited for; matrix products, arithmetic and copies ran while one was open for 1% of the time, Pallas kernels for 0%

profile of v1, /device:TPU:1, one launch (start us, length us, event | category | flops | bytes accessed | tf_op | source)
XLA Modules:
  0.0 380.0 jit_solution(16325157703490130457)
XLA Ops:
  3.5 27.1 %all_gather.3 = bf16[64,4096]{1,0:T(8,128)(2,1)S(1)} all-gather(bf16[64,512]{1,0:T(8,128)(2,1)} %param.6), channel_id=1, replica_groups=mesh['expert'=64,'hidden'=8] {'hidden'}, dimensions={1}, use_global_device_ids=true | all-gather | bytes 589824 | tf_op jit(solution)/shard_map/all_gather | solution.py:41
  30.7 4.4 %gather_fusion = bf16[512,4096]{1,0:T(8,128)(2,1)} fusion(bf16[64,4096]{1,0:T(8,128)(2,1)S(1)} %all_gather.3, s32[1024]{0:T(1024)S(1)} %pad_clamp_fusion.1), kind=kCustom, calls=%fused_computation | custom fusion | bytes 8390656 | tf_op jit(solution)/shard_map/gather | solution.py:43
  35.1 12.4 %scatter_custom_fusion = bf16[1024,4096]{1,0:T(8,128)(2,1)} fusion(s32[512]{0:T(512)S(1)} %bitcast.90, bf16[512,4096]{1,0:T(8,128)(2,1)} %gather_fusion, bf16[]{:T(256)} %constant.81.clone.1), kind=kCustom, calls=%fused_computation.3 | custom fusion | bytes 8389120 | tf_op jit(solution)/shard_map/scatter | solution.py:43
  47.5 16.7 %all-to-all-start = ((bf16[64,16,4096]{2,1,0:T(8,128)(2,1)}), bf16[64,16,4096]{2,1,0:T(8,128)(2,1)}, u32[]{:S(2)}, u32[]{:S(2)}) async-start(bf16[64,16,4096]{2,1,0:T(8,128)(2,1)} %bitcast.85), calls=%async_computation | async-start | bytes 16777216 | tf_op jit(solution)/shard_map/all_to_all | solution.py:44
  64.2 182.4 %all-to-all-done = bf16[64,16,4096]{2,1,0:T(8,128)(2,1)} async-done(((bf16[64,16,4096]{2,1,0:T(8,128)(2,1)}), bf16[64,16,4096]{2,1,0:T(8,128)(2,1)}, u32[]{:S(2)}, u32[]{:S(2)}) %all-to-all-start) | async-done | bytes 8388640 | tf_op jit(solution)/shard_map/all_to_all | solution.py:44
  246.6 6.7 %fusion.14 = f32[192,1024]{1,0:T(8,128)S(1)} fusion(bf16[1024,4096]{1,0:T(8,128)(2,1)} %bitcast.5, bf16[1,192,4096]{2,1,0:T(8,128)(2,1)} %param.9), kind=kOutput, calls=%fused_computation.13 | convolution fusion | flops 1610612736 | bytes 10747904 | tf_op jit(solution)/shard_map/lrd,lfd->lfr/dot_general | solution.py:51
  253.3 2.2 broadcast.119
  255.5 7.1 %constant_dynamic-update-slice_fusion = (bf16[1536,1024]{1,0:T(8,128)(2,1)}, bf16[192,1024]{1,0:T(8,128)(2,1)S(1)}) fusion(bf16[1536,1024]{1,0:T(8,128)(2,1)} %broadcast.119, s32[]{:T(128)S(6)} %select_n.91, bf16[1024,4096]{1,0:T(8,128)(2,1)} %bitcast.5, bf16[1,192,4096]{2,1,0:T(8,128)(2,1)S(1)} %copy-done, f32[192,1024]{1,0:T(8,128)S(1)} %fusion.14), kind=kOutput, calls=%fused_computation.44 | convolution fusion | flops 1611792384 | bytes 11534340 | tf_op jit(solution)/shard_map/lrd,lfd->lfr/dot_general | solution.py:52
  262.6 3.4 collective-permute-start
  266.0 3.1 collective-permute-start.1
  269.2 3.1 collective-permute-done
  272.3 2.2 collective-permute-start.2
  274.8 4.0 %collective-permute-start.3 = (bf16[1,192,1024]{2,1,0:T(8,128)(2,1)S(1)}, bf16[1,192,1024]{2,1,0:T(8,128)(2,1)S(1)}, u32[]{:S(2)}, u32[]{:S(2)}) collective-permute-start(bf16[1,192,1024]{2,1,0:T(8,128)(2,1)S(1)} %collective-permute-done.1), channel_id=1, source_target_pairs={{0,7},{1,0},{2,1},{3,2},{4,3},{5,4},{6,5},{7,6},{8,15},{9,8},{10,9... | collective-permute-start | bytes 1179656 | tf_op jit(solution)/shard_map/ppermute | solution.py:21
  282.0 1.9 collective-permute-start.4
  284.0 4.6 %collective-permute-start.5 = (bf16[1,192,1024]{2,1,0:T(8,128)(2,1)S(1)}, bf16[1,192,1024]{2,1,0:T(8,128)(2,1)S(1)}, u32[]{:S(2)}, u32[]{:S(2)}) collective-permute-start(bf16[1,192,1024]{2,1,0:T(8,128)(2,1)S(1)} %collective-permute-done.3), channel_id=1, source_target_pairs={{0,7},{1,0},{2,1},{3,2},{4,3},{5,4},{6,5},{7,6},{8,15},{9,8},{10,9... | collective-permute-start | bytes 1179656 | tf_op jit(solution)/shard_map/ppermute | solution.py:21
  292.1 1.9 collective-permute-start.6
  295.6 7.6 %collective-permute-done.6 = bf16[1,192,1024]{2,1,0:T(8,128)(2,1)S(1)} collective-permute-done((bf16[1,192,1024]{2,1,0:T(8,128)(2,1)S(1)}, bf16[1,192,1024]{2,1,0:T(8,128)(2,1)S(1)}, u32[]{:S(2)}, u32[]{:S(2)}) %collective-permute-start.6) | collective-permute-done | bytes 393248 | tf_op jit(solution)/shard_map/ppermute | solution.py:16
  303.9 3.7 fusion.11
  307.7 3.0 copy.31
  311.2 8.0 %reduce.2 = bf16[1024,512]{1,0:T(8,128)(2,1)S(1)} reduce(bf16[1024,1,512]{2,1,0:T(2,128)(2,1)} %bitcast.88, bf16[]{:T(256)} %broadcast.141), dimensions={1}, to_apply=%bitcast.84.reduce_sub_computation | reduce | bytes 2097154
  320.8 22.9 %all-to-all-start.1 = ((bf16[64,2,4096]{2,1,0:T(2,128)(2,1)}), bf16[64,2,4096]{2,1,0:T(2,128)(2,1)S(1)}, u32[]{:S(2)}, u32[]{:S(2)}) async-start(bf16[64,2,4096]{2,1,0:T(2,128)(2,1)} %reshape.206), calls=%async_computation.1 | async-start | bytes 2097152 | tf_op jit(solution)/shard_map/all_to_all | solution.py:60
  343.8 27.9 %all-to-all-done.1 = bf16[64,2,4096]{2,1,0:T(2,128)(2,1)S(1)} async-done(((bf16[64,2,4096]{2,1,0:T(2,128)(2,1)}), bf16[64,2,4096]{2,1,0:T(2,128)(2,1)S(1)}, u32[]{:S(2)}, u32[]{:S(2)}) %all-to-all-start.1) | async-done | bytes 1048608 | tf_op jit(solution)/shard_map/all_to_all | solution.py:60
  371.7 3.5 reshape.207
  377.1 2.0 gather_fusion.1
  (39 shorter events, 18.1 us)
Async XLA Ops:
  0.0 255.5 %copy-start = (bf16[1,192,4096]{2,1,0:T(8,128)(2,1)S(1)}, bf16[1,192,4096]{2,1,0:T(8,128)(2,1)}, u32[]{:S(2)}) copy-start(bf16[1,192,4096]{2,1,0:T(8,128)(2,1)} %param.10) | copy-start | bytes 4718596
  47.5 199.1 %all-to-all-start = ((bf16[64,16,4096]{2,1,0:T(8,128)(2,1)}), bf16[64,16,4096]{2,1,0:T(8,128)(2,1)}, u32[]{:S(2)}, u32[]{:S(2)}) async-start(bf16[64,16,4096]{2,1,0:T(8,128)(2,1)} %bitcast.85), calls=%async_computation | async-start | bytes 16777216 | tf_op jit(solution)/shard_map/all_to_all | solution.py:44
  262.6 9.7 %collective-permute-start = (bf16[1,192,1024]{2,1,0:T(8,128)(2,1)S(1)}, bf16[1,192,1024]{2,1,0:T(8,128)(2,1)S(1)}, u32[]{:S(2)}, u32[]{:S(2)}) collective-permute-start(bf16[1,192,1024]{2,1,0:T(8,128)(2,1)S(1)} %bitcast.93), channel_id=1, source_target_pairs={{0,1},{1,2},{2,3},{3,4},{4,5},{5,6},{6,7},{7,0},{8,9},{9,10},{10,1... | collective-permute-start | bytes 1179656 | tf_op jit(solution)/shard_map/ppermute | solution.py:16
  266.0 8.8 %collective-permute-start.1 = (bf16[1,192,1024]{2,1,0:T(8,128)(2,1)S(1)}, bf16[1,192,1024]{2,1,0:T(8,128)(2,1)S(1)}, u32[]{:S(2)}, u32[]{:S(2)}) collective-permute-start(bf16[1,192,1024]{2,1,0:T(8,128)(2,1)S(1)} %bitcast.94), channel_id=1, source_target_pairs={{0,7},{1,0},{2,1},{3,2},{4,3},{5,4},{6,5},{7,6},{8,15},{9,8},{10,9... | collective-permute-start | bytes 1179656 | tf_op jit(solution)/shard_map/ppermute | solution.py:21
  269.2 34.7 %copy-start.2 = (bf16[1,1536,512]{2,1,0:T(8,128)(2,1)S(1)}, bf16[1,1536,512]{2,1,0:T(8,128)(2,1)}, u32[]{:S(2)}) copy-start(bf16[1,1536,512]{2,1,0:T(8,128)(2,1)} %param.11) | copy-start | bytes 4718596
  272.3 9.7 %collective-permute-start.2 = (bf16[1,192,1024]{2,1,0:T(8,128)(2,1)S(1)}, bf16[1,192,1024]{2,1,0:T(8,128)(2,1)S(1)}, u32[]{:S(2)}, u32[]{:S(2)}) collective-permute-start(bf16[1,192,1024]{2,1,0:T(8,128)(2,1)S(1)} %collective-permute-done), channel_id=1, source_target_pairs={{0,1},{1,2},{2,3},{3,4},{4,5},{5,6},{6,7},{7,0},{8,9},{9,10},{10,1... | collective-permute-start | bytes 1179656 | tf_op jit(solution)/shard_map/ppermute | solution.py:16
  274.8 9.2 %collective-permute-start.3 = (bf16[1,192,1024]{2,1,0:T(8,128)(2,1)S(1)}, bf16[1,192,1024]{2,1,0:T(8,128)(2,1)S(1)}, u32[]{:S(2)}, u32[]{:S(2)}) collective-permute-start(bf16[1,192,1024]{2,1,0:T(8,128)(2,1)S(1)} %collective-permute-done.1), channel_id=1, source_target_pairs={{0,7},{1,0},{2,1},{3,2},{4,3},{5,4},{6,5},{7,6},{8,15},{9,8},{10,9... | collective-permute-start | bytes 1179656 | tf_op jit(solution)/shard_map/ppermute | solution.py:21
  282.0 10.0 %collective-permute-start.4 = (bf16[1,192,1024]{2,1,0:T(8,128)(2,1)S(1)}, bf16[1,192,1024]{2,1,0:T(8,128)(2,1)S(1)}, u32[]{:S(2)}, u32[]{:S(2)}) collective-permute-start(bf16[1,192,1024]{2,1,0:T(8,128)(2,1)S(1)} %collective-permute-done.2), channel_id=1, source_target_pairs={{0,1},{1,2},{2,3},{3,4},{4,5},{5,6},{6,7},{7,0},{8,9},{9,10},{10,1... | collective-permute-start | bytes 1179656 | tf_op jit(solution)/shard_map/ppermute | solution.py:16
  284.0 10.8 %collective-permute-start.5 = (bf16[1,192,1024]{2,1,0:T(8,128)(2,1)S(1)}, bf16[1,192,1024]{2,1,0:T(8,128)(2,1)S(1)}, u32[]{:S(2)}, u32[]{:S(2)}) collective-permute-start(bf16[1,192,1024]{2,1,0:T(8,128)(2,1)S(1)} %collective-permute-done.3), channel_id=1, source_target_pairs={{0,7},{1,0},{2,1},{3,2},{4,3},{5,4},{6,5},{7,6},{8,15},{9,8},{10,9... | collective-permute-start | bytes 1179656 | tf_op jit(solution)/shard_map/ppermute | solution.py:21
  292.1 11.1 %collective-permute-start.6 = (bf16[1,192,1024]{2,1,0:T(8,128)(2,1)S(1)}, bf16[1,192,1024]{2,1,0:T(8,128)(2,1)S(1)}, u32[]{:S(2)}, u32[]{:S(2)}) collective-permute-start(bf16[1,192,1024]{2,1,0:T(8,128)(2,1)S(1)} %collective-permute-done.4), channel_id=1, source_target_pairs={{0,1},{1,2},{2,3},{3,4},{4,5},{5,6},{6,7},{7,0},{8,9},{9,10},{10,1... | collective-permute-start | bytes 1179656 | tf_op jit(solution)/shard_map/ppermute | solution.py:16
  311.2 32.6 %copy-start.1 = (f32[64,8]{0,1:T(8,128)S(1)}, f32[64,8]{0,1:T(8,128)}, u32[]{:S(2)}) copy-start(f32[64,8]{0,1:T(8,128)} %param.8) | copy-start | bytes 6148
  320.8 50.9 %all-to-all-start.1 = ((bf16[64,2,4096]{2,1,0:T(2,128)(2,1)}), bf16[64,2,4096]{2,1,0:T(2,128)(2,1)S(1)}, u32[]{:S(2)}, u32[]{:S(2)}) async-start(bf16[64,2,4096]{2,1,0:T(2,128)(2,1)} %reshape.206), calls=%async_computation.1 | async-start | bytes 2097152 | tf_op jit(solution)/shard_map/all_to_all | solution.py:60
